TPU v7x, 32 devices: a whole 2x2x4 slice. The times are simulated.
32 devices in a mesh: cols: 32 (over z, y, x, core).
Axes of the slice: x: 2, y: 2, z: 4, core: 2. Of those that a mesh axis runs over, the one named last changes fastest.
Arguments:
- gcm_state: float32 [2, 72, 16384], P(None, None, 'cols'), may hold values from -6 to 6
- crm_state: bfloat16 [2, 58, 32, 16384], P(None, None, None, 'cols'), may hold values from -6 to 6
- span_map: int32 [16384], P('cols'), may hold values from 0 to 16383, as said below
- crm_cost: int32 [16384], P('cols'), may hold values from 1 to 58
- neighbours: int32 [4096, 8], P('cols'), may hold values from -1 to 4095, as said below
Outputs:
- crm_next: bfloat16 [2, 58, 32, 16384], P(None, None, None, 'cols')
- smoothed: float32 [2, 72, 16384], P(None, None, 'cols')
Inputs may be any that keep to these rules, and one draw needn't show every extreme that they name: `span_map`: A permutation of the span positions; position p is held by device p // 512. The columns of each device go, exactly 32 each, to 16 distinct devices, its own among them, and each device receives exactly 32 columns from each of 16 devices. `neighbours`: -1 marks an empty slot and stands only in the last slot; every other entry names an element of the element's own device or of one of the two devices beside it along cols, wrapping around.
All inputs are finite; a program needn't handle non-finite values.
Results may differ from a plain program's by a relative error of at most 0.001.
Values sent between devices are 32-bit elements; how exact they have to be, the bound alone decides.
A program may use at most 128 MiB of HBM per device.

v0:
```python
import jax
import jax.numpy as jnp
from jax import lax
from jax.sharding import PartitionSpec as P

LEV = 72
CRM_LEV = 58
PCOL = 4
NBR = 8
SUBSTEPS = 2
RELAX = 0.5
STEP = 0.5
MIXING = 0.2
LATENT = 0.6
SMOOTHING = 0.5


def padded(shard, sides, width):
    for axis, dim in sides:
        size, length = (lax.axis_size(axis), shard.shape[dim])
        up = [(i, (i + 1) % size) for i in range(size)]
        down = [(j, i) for i, j in up]
        last = lax.slice_in_dim(shard, length - width, length, axis=dim)
        first = lax.slice_in_dim(shard, 0, width, axis=dim)
        before = lax.ppermute(last, axis, up)
        after = lax.ppermute(first, axis, down)
        shard = jnp.concatenate([before, shard, after], axis=dim)
    return shard


def interpolation(rows_out, rows_in):
    target = jnp.arange(rows_out, dtype=jnp.int32)[:, None]
    source = jnp.arange(rows_in, dtype=jnp.int32)[None, :]
    scaled = target * (rows_in - 1)
    lower = scaled // (rows_out - 1)
    weight = (scaled - lower * (rows_out - 1)).astype(jnp.float32) / (rows_out - 1)
    upper = jnp.minimum(lower + 1, rows_in - 1)
    return jnp.where(source == lower, 1.0 - weight, 0.0) + jnp.where(source == upper, weight, 0.0)


def crm_steps(fields, forcing, active):
    levels = fields.shape[1]
    height = jnp.arange(levels, dtype=jnp.float32)
    saturation = (1.0 - 0.8 * height / (levels - 1))[:, None, None]
    for substep in range(SUBSTEPS):
        sideways = jnp.roll(fields, 1, axis=2) + jnp.roll(fields, -1, axis=2) - 2.0 * fields
        upper_cells = jnp.concatenate([fields[:, 1:], fields[:, -1:]], axis=1)
        lower_cells = jnp.concatenate([fields[:, :1], fields[:, :-1]], axis=1)
        vertical = upper_cells + lower_cells - 2.0 * fields
        fields = fields + STEP * (forcing[:, :, None, :] + MIXING * (sideways + vertical))
        condensed = jnp.maximum(fields[1] - saturation, 0.0) * active[:, None, :]
        fields = jnp.stack([fields[0] + LATENT * condensed, fields[1] - condensed])
    return fields


def physics(crm_old, profile, cloud_top):
    start = crm_old.astype(jnp.float32)
    start_mean = jnp.mean(start, axis=2)
    forcing = RELAX * (profile - start_mean)
    levels = crm_old.shape[1]
    active = (jnp.arange(levels, dtype=jnp.int32)[:, None] < cloud_top[None, :]).astype(jnp.float32)
    final = crm_steps(start, forcing, active)
    change = jnp.mean(final, axis=2) - start_mean
    return (final.astype(jnp.bfloat16), change)


def element_mean(values, elements):
    return jnp.mean(values.reshape(2 * LEV, elements, PCOL), axis=2)


def on_device(gcm_state, crm_state, span_map, crm_cost, neighbours):
    devices = lax.axis_size("cols")
    device = lax.axis_index("cols")
    columns = gcm_state.shape[2]
    elements = neighbours.shape[0]
    capacity = 2 * columns // devices
    interp_down = interpolation(CRM_LEV, LEV)
    interp_up = interpolation(LEV, CRM_LEV)
    target = span_map // columns
    span_slot = span_map % columns
    peer_ids = jnp.arange(devices, dtype=jnp.int32)
    onehot = (target[:, None] == peer_ids[None, :]).astype(jnp.int32)
    before = jnp.cumsum(onehot, axis=0) - onehot
    within = jnp.sum(before * onehot, axis=1)
    position = target * capacity + within
    outgoing = gcm_state.reshape(2 * LEV, columns)
    row_count = outgoing.shape[0]
    slot_total = devices * capacity
    send_rows = jnp.zeros((row_count, slot_total), jnp.float32).at[:, position].set(outgoing)
    labels = jnp.stack([span_slot, crm_cost]).astype(jnp.float32)
    empty_labels = jnp.stack(
        [jnp.full((slot_total,), columns, jnp.float32), jnp.zeros((slot_total,), jnp.float32)]
    )
    send_labels = empty_labels.at[:, position].set(labels)
    arrived, arrived_labels = (
        lax.all_to_all(send_rows, "cols", split_axis=1, concat_axis=1, tiled=True),
        lax.all_to_all(send_labels, "cols", split_axis=1, concat_axis=1, tiled=True),
    )
    arrived_slot = arrived_labels[0].astype(jnp.int32)
    placed = (
        jnp.zeros((row_count, columns + 1), jnp.float32)
        .at[:, arrived_slot]
        .set(arrived)[:, :columns]
    )
    span_top = (
        jnp.zeros((columns + 1,), jnp.int32)
        .at[arrived_slot]
        .set(arrived_labels[1].astype(jnp.int32))[:columns]
    )
    span_profile = jnp.einsum(
        "jk,fkc->fjc", interp_down, placed.reshape(2, LEV, columns), precision=lax.Precision.HIGHEST
    )
    crm_next, change = physics(crm_state, span_profile, span_top)
    returning = jnp.einsum(
        "kj,fjc->fkc", interp_up, change, precision=lax.Precision.HIGHEST
    ).reshape(2 * LEV, columns)
    source_slot = jnp.minimum(arrived_slot, columns - 1)
    returned = lax.all_to_all(
        returning[:, source_slot], "cols", split_axis=1, concat_axis=1, tiled=True
    )
    own_rows = returned[:, position]
    tendency = own_rows.reshape(2, LEV, columns)
    updated = gcm_state + tendency
    edge_mean = element_mean(updated, elements)
    extended = padded(edge_mean, (("cols", 1),), elements)
    valid = neighbours >= 0
    offset = jnp.mod(neighbours - (device - 1) * elements, devices * elements)
    lookup = jnp.where(valid, offset, 0)
    gathered = jnp.take(extended, lookup.reshape(-1), axis=1).reshape(2 * LEV, elements, NBR)
    gathered = gathered * valid.astype(jnp.float32)[None]
    neighbour_sum = jnp.sum(gathered, axis=2)
    count = jnp.sum(valid.astype(jnp.float32), axis=1)
    pull = SMOOTHING * (neighbour_sum / count[None, :] - edge_mean)
    smoothed = (updated.reshape(2 * LEV, elements, PCOL) + pull[:, :, None]).reshape(
        2, LEV, columns
    )
    return (crm_next, smoothed)


def solution(mesh):
    placed = (
        P(None, None, "cols"),
        P(None, None, None, "cols"),
        P("cols"),
        P("cols"),
        P("cols", None),
    )
    return jax.shard_map(
        on_device,
        mesh=mesh,
        in_specs=placed,
        out_specs=(P(None, None, None, "cols"), P(None, None, "cols")),
        check_vma=False,
    )
```

profile of v0, /device:TPU:0, one launch (start us, length us, event | category | flops | bytes accessed | tf_op | source)
XLA Modules:
  0.0 169.9 jit_solution(7699775522284530339)
XLA Ops:
  0.6 0.7 add_select_fusion.1
  1.3 1.2 reduce-window.6
  2.5 0.2 slice_reduce_fusion
  2.8 0.1 fusion.43
  2.9 0.7 fusion.67
  3.6 0.1 copy.27
  3.7 1.0 copy.42
  4.8 1.9 %scatter_fusion = f32[2,1024]{0,1:T(8,128)S(1)} fusion(f32[2,1024]{0,1:T(8,128)S(1)} %copy.42, s32[512]{0:T(512)S(1)} %compare_select_fusion.4, f32[512,2]{1,0:T(8,128)S(1)} %copy.27), kind=kCustom, calls=%fused_computation.3 | custom fusion | bytes 14336 | tf_op jit(solution)/shard_map/scatter | solution.py:94
  6.7 0.9 copy.28
  7.6 7.3 %all-to-all-start = ((f32[2,32,32]{2,0,1:T(2,128)}), f32[2,32,32]{2,0,1:T(2,128)S(1)}, u32[]{:S(2)}, u32[]{:S(2)}) async-start(f32[2,32,32]{2,0,1:T(2,128)} %copy.28), calls=%async_computation | async-start | bytes 65536 | tf_op jit(solution)/shard_map/all_to_all | solution.py:97
  14.9 0.0 copy-start
  14.9 11.3 %fusion.79 = (f32[2,58,31,512]{3,2,1,0:T(8,128)}, f32[2,58,31,512]{3,2,1,0:T(8,128)}) fusion(bf16[2,58,32,512]{3,2,1,0:T(8,128)(2,1)} %param.6), kind=kLoop, calls=%fused_computation.161 | loop fusion | bytes 29458432 | tf_op jit(solution)/shard_map/jit(_roll_static)/slice | solution.py:46
  26.2 7.3 %fusion.78 = (f32[2,57,32,512]{3,2,1,0:T(8,128)}, f32[2,57,32,512]{3,2,1,0:T(8,128)}) fusion(bf16[2,58,32,512]{3,2,1,0:T(8,128)(2,1)S(1)} %copy-done), kind=kLoop, calls=%fused_computation.160 | loop fusion | bytes 29884416 | tf_op jit(solution)/shard_map/slice | solution.py:48
  33.5 0.3 fusion.80
  33.9 0.2 copy.29
  34.1 3.3 %scatter_custom_fusion.1 = f32[144,1024]{0,1:T(8,128)} fusion(s32[512]{0:T(512)S(1)} %compare_select_fusion.4, f32[144,512]{0,1:T(8,128)S(1)} %copy.29, f32[]{:T(128)} %constant.56.clone.1), kind=kCustom, calls=%fused_computation.62 | custom fusion | bytes 1114116 | tf_op jit(solution)/shard_map/scatter | solution.py:89
  37.4 0.0 all-to-all-done
  37.4 5.8 %all-to-all-start.1 = ((f32[144,32,32]{0,2,1:T(8,128)}), f32[144,32,32]{0,2,1:T(8,128)S(1)}, u32[]{:S(2)}, u32[]{:S(2)}) async-start(f32[144,32,32]{0,2,1:T(8,128)} %bitcast.9), calls=%async_computation.1 | async-start | bytes 2097152 | tf_op jit(solution)/shard_map/all_to_all | solution.py:96
  43.3 3.4 %convert_reduce_fusion = f32[2,58,512]{2,1,0:T(8,128)S(1)} fusion(bf16[2,58,32,512]{3,2,1,0:T(8,128)(2,1)} %param.6), kind=kLoop, calls=%fused_computation.55 | loop fusion | flops 3741696 | bytes 4038656 | tf_op jit(solution)/shard_map/reduce_sum | solution.py:58
  46.7 0.1 fusion.53
  46.8 0.1 convert_element_type.77
  46.9 0.1 reshape.308
  46.9 4.3 %scatter_custom_fusion.3 = s32[513]{0:T(1024)S(1)} fusion(s32[1024]{0:T(1024)S(1)} %bitcast.83, s32[1024]{0:T(1024)S(1)} %reshape.308, s32[]{:T(128)} %constant.62.clone.1), kind=kCustom, calls=%fused_computation.139 | custom fusion | bytes 2056 | tf_op jit(solution)/shard_map/scatter | solution.py:108
  51.3 18.2 %all-to-all-done.1 = f32[144,32,32]{0,2,1:T(8,128)S(1)} async-done(((f32[144,32,32]{0,2,1:T(8,128)}), f32[144,32,32]{0,2,1:T(8,128)S(1)}, u32[]{:S(2)}, u32[]{:S(2)}) %all-to-all-start.1) | async-done | bytes 589856 | tf_op jit(solution)/shard_map/all_to_all | solution.py:96
  69.5 5.1 %scatter_custom_fusion.2 = f32[144,513]{0,1:T(8,128)S(1)} fusion(s32[1024]{0:T(1024)S(1)} %bitcast.84, f32[1024,144]{1,0:T(8,128)S(1)} %bitcast.78, f32[]{:T(128)} %constant.56.clone.1), kind=kCustom, calls=%fused_computation.66 | custom fusion | bytes 295492 | tf_op jit(solution)/shard_map/scatter | solution.py:103
  74.6 0.2 copy.30
  74.8 0.4 fusion.23
  75.2 13.5 %fusion.7 = f32[2,58,32,512]{3,2,1,0:T(8,128)S(1)} fusion(f32[2,58,31,512]{3,2,1,0:T(8,128)} %get-tuple-element.23, f32[2,58,1,512]{3,2,1,0:T(1,128)S(1)} %get-tuple-element.25, f32[2,58,1,512]{3,2,1,0:T(1,128)S(1)} %get-tuple-element.24, f32[2,58,31,512]{3,2,1,0:T(8,128)} %get-tuple-element.22, f32[2,1,32,512]{3,2,1,0:T(8,128)S(1)} %get-tuple-element.19, ...), kind=kLoop, calls=%fused_computation.32 | loop fusion | flops 28508160 | bytes 42049536 | tf_op jit(solution)/shard_map/add | solution.py:50
  88.8 1.5 fusion.21
  90.3 6.1 %fusion.17 = (f32[2,57,32,512]{3,2,1,0:T(8,128)}, f32[2,57,32,512]{3,2,1,0:T(8,128)}) fusion(f32[1,58,32,512]{3,2,1,0:T(8,128)S(1)} %get-tuple-element.9, f32[1,58,32,512]{3,2,1,0:T(8,128)S(1)} %get-tuple-element.8), kind=kLoop, calls=%fused_computation.46 | loop fusion | flops 3735552 | bytes 22544384 | tf_op jit(solution)/shard_map/stack | solution.py:52
  96.4 0.5 fusion.36
  96.8 4.0 %fusion.1 = (f32[2,58,31,512]{3,2,1,0:T(8,128)S(1)}, f32[2,58,31,512]{3,2,1,0:T(8,128)}) fusion(f32[1,58,32,512]{3,2,1,0:T(8,128)S(1)} %get-tuple-element.9, f32[1,58,32,512]{3,2,1,0:T(8,128)S(1)} %get-tuple-element.8), kind=kLoop, calls=%fused_computation.25 | loop fusion | flops 3682304 | bytes 22331392 | tf_op jit(solution)/shard_map/stack | solution.py:52
  100.9 9.7 %fusion.14 = f32[2,58,32,512]{3,2,1,0:T(8,128)S(1)} fusion(f32[2,58,31,512]{3,2,1,0:T(8,128)} %get-tuple-element.15, f32[2,58,1,512]{3,2,1,0:T(1,128)S(1)} %get-tuple-element.17, f32[2,58,1,512]{3,2,1,0:T(1,128)S(1)} %get-tuple-element.16, f32[2,58,31,512]{3,2,1,0:T(8,128)S(1)} %get-tuple-element.14, f32[1,58,32,512]{3,2,1,0:T(8,128)S(1)} %get-tuple-element.8, ...), kind=kLoop, calls=%fused_computation.41 | loop fusion | flops 28508160 | bytes 45850624 | tf_op jit(solution)/shard_map/add | solution.py:50
  110.5 1.9 %slice_add_fusion = (f32[1,58,32,512]{3,2,1,0:T(8,128)S(1)}, f32[1,58,32,512]{3,2,1,0:T(8,128)S(1)}) fusion(f32[2,58,32,512]{3,2,1,0:T(8,128)S(1)} %fusion.14, f32[58,512]{1,0:T(8,128)S(1)} %fusion.40, f32[58]{0:T(128)S(1)} %multiply_subtract_fusion), kind=kLoop, calls=%fused_computation.49 | loop fusion | flops 5701632 | bytes 15323368 | tf_op jit(solution)/shard_map/add | solution.py:52
  112.5 0.0 copy-start.4
  112.5 1.5 fusion.18
  114.0 0.4 fusion.31
  114.5 0.9 copy-done.2
  115.4 0.2 copy.31
  115.6 4.7 %gather_fusion = f32[1024,144]{1,0:T(8,128)} fusion(f32[144,512]{0,1:T(8,128)S(1)} %copy.31, s32[1024]{0:T(1024)S(1)} %broadcast_clamp_fusion.1), kind=kCustom, calls=%fused_computation | custom fusion | bytes 1183744 | tf_op jit(solution)/shard_map/gather | solution.py:119
  120.3 3.8 %all-to-all-start.2 = ((f32[144,32,32]{0,2,1:T(8,128)}), f32[144,32,32]{0,2,1:T(8,128)S(1)}, u32[]{:S(2)}, u32[]{:S(2)}) async-start(f32[144,32,32]{0,2,1:T(8,128)} %bitcast.20), calls=%async_computation.2 | async-start | bytes 2097152 | tf_op jit(solution)/shard_map/all_to_all | solution.py:118
  124.2 0.1 copy.35
  124.3 0.1 reshape.255
  124.4 0.1 copy.36
  124.5 0.1 copy.33
  124.6 25.5 %all-to-all-done.2 = f32[144,32,32]{0,2,1:T(8,128)S(1)} async-done(((f32[144,32,32]{0,2,1:T(8,128)}), f32[144,32,32]{0,2,1:T(8,128)S(1)}, u32[]{:S(2)}, u32[]{:S(2)}) %all-to-all-start.2) | async-done | bytes 589856 | tf_op jit(solution)/shard_map/all_to_all | solution.py:118
  150.1 1.6 gather_fusion.1
  151.7 0.2 copy.32
  151.9 0.1 add.205
  151.9 0.2 copy.34
  152.2 0.4 reshape.254
  152.6 0.3 reduce_sum.57
  153.0 0.1 collective-permute-start
  153.0 5.3 %collective-permute-start.1 = (f32[144,128]{0,1:T(8,128)S(1)}, f32[144,128]{0,1:T(8,128)S(1)}, u32[]{:S(2)}, u32[]{:S(2)}) collective-permute-start(f32[144,128]{0,1:T(8,128)S(1)} %broadcast_multiply_fusion), channel_id=1, source_target_pairs={{1,0},{2,1},{3,2},{4,3},{5,4},{6,5},{7,6},{8,7},{9,8},{10,9},{11,1... | collective-permute-start | bytes 221192 | tf_op jit(solution)/shard_map/ppermute | solution.py:26
  158.4 5.8 %fusion.19 = bf16[2,58,32,512]{3,2,1,0:T(8,128)(2,1)} fusion(f32[1,58,32,512]{3,2,1,0:T(8,128)} %copy-done.2, f32[1,58,32,512]{3,2,1,0:T(8,128)} %copy-done.1), kind=kLoop, calls=%fused_computation.48 | loop fusion | flops 1900544 | bytes 11403264 | tf_op jit(solution)/shard_map/convert_element_type | solution.py:64
  164.1 0.0 collective-permute-done
  164.1 0.0 collective-permute-done.1
  164.2 3.5 %gather_fusion.2 = f32[1024,144]{1,0:T(8,128)S(1)} fusion(f32[144,384]{0,1:T(8,128)S(1)} %pad_maximum_fusion.2, s32[1024]{0:T(1024)S(1)} %broadcast_clamp_fusion), kind=kCustom, calls=%fused_computation.2 | custom fusion | bytes 1183744 | tf_op jit(solution)/shard_map/jit(_take)/gather | solution.py:129
  167.6 0.7 fusion.25
  168.3 0.1 subtract_multiply_fusion
  168.4 0.1 add.211
  168.5 0.5 add.212
  169.0 0.2 copy.37
  169.2 0.8 add.213
  (30 shorter events, 0.4 us)
Async XLA Ops:
  7.6 29.8 %all-to-all-start = ((f32[2,32,32]{2,0,1:T(2,128)}), f32[2,32,32]{2,0,1:T(2,128)S(1)}, u32[]{:S(2)}, u32[]{:S(2)}) async-start(f32[2,32,32]{2,0,1:T(2,128)} %copy.28), calls=%async_computation | async-start | bytes 65536 | tf_op jit(solution)/shard_map/all_to_all | solution.py:97
  14.9 11.3 %copy-start = (bf16[2,58,32,512]{3,2,1,0:T(8,128)(2,1)S(1)}, bf16[2,58,32,512]{3,2,1,0:T(8,128)(2,1)}, u32[]{:S(2)}) copy-start(bf16[2,58,32,512]{3,2,1,0:T(8,128)(2,1)} %param.6) | copy-start | bytes 11403268
  26.2 7.7 %copy-start.3 = (f32[2,72,512]{2,1,0:T(8,128)S(1)}, f32[2,72,512]{2,1,0:T(8,128)}, u32[]{:S(2)}) copy-start(f32[2,72,512]{2,1,0:T(8,128)} %param.5) | copy-start | bytes 884740
  37.4 32.1 %all-to-all-start.1 = ((f32[144,32,32]{0,2,1:T(8,128)}), f32[144,32,32]{0,2,1:T(8,128)S(1)}, u32[]{:S(2)}, u32[]{:S(2)}) async-start(f32[144,32,32]{0,2,1:T(8,128)} %bitcast.9), calls=%async_computation.1 | async-start | bytes 2097152 | tf_op jit(solution)/shard_map/all_to_all | solution.py:96
  112.4 2.0 %copy-start.1 = (f32[1,58,32,512]{3,2,1,0:T(8,128)}, f32[1,58,32,512]{3,2,1,0:T(8,128)S(1)}, u32[]{:S(2)}) copy-start(f32[1,58,32,512]{3,2,1,0:T(8,128)S(1)} %get-tuple-element.6) | copy-start | bytes 11403268
  112.5 2.9 %copy-start.2 = (f32[1,58,32,512]{3,2,1,0:T(8,128)}, f32[1,58,32,512]{3,2,1,0:T(8,128)S(1)}, u32[]{:S(2)}) copy-start(f32[1,58,32,512]{3,2,1,0:T(8,128)S(1)} %get-tuple-element.7) | copy-start | bytes 11403268
  112.5 11.7 %copy-start.4 = (s32[128,8]{0,1:T(8,128)S(1)}, s32[128,8]{0,1:T(8,128)}, u32[]{:S(2)}) copy-start(s32[128,8]{0,1:T(8,128)} %param.9) | copy-start | bytes 12292
  120.3 29.9 %all-to-all-start.2 = ((f32[144,32,32]{0,2,1:T(8,128)}), f32[144,32,32]{0,2,1:T(8,128)S(1)}, u32[]{:S(2)}, u32[]{:S(2)}) async-start(f32[144,32,32]{0,2,1:T(8,128)} %bitcast.20), calls=%async_computation.2 | async-start | bytes 2097152 | tf_op jit(solution)/shard_map/all_to_all | solution.py:118
  153.0 11.2 %collective-permute-start = (f32[144,128]{0,1:T(8,128)S(1)}, f32[144,128]{0,1:T(8,128)S(1)}, u32[]{:S(2)}, u32[]{:S(2)}) collective-permute-start(f32[144,128]{0,1:T(8,128)S(1)} %broadcast_multiply_fusion), channel_id=1, source_target_pairs={{0,1},{1,2},{2,3},{3,4},{4,5},{5,6},{6,7},{7,8},{8,9},{9,10},{10,1... | collective-permute-start | bytes 221192 | tf_op jit(solution)/shard_map/ppermute | solution.py:25
  153.0 11.1 %collective-permute-start.1 = (f32[144,128]{0,1:T(8,128)S(1)}, f32[144,128]{0,1:T(8,128)S(1)}, u32[]{:S(2)}, u32[]{:S(2)}) collective-permute-start(f32[144,128]{0,1:T(8,128)S(1)} %broadcast_multiply_fusion), channel_id=1, source_target_pairs={{1,0},{2,1},{3,2},{4,3},{5,4},{6,5},{7,6},{8,7},{9,8},{10,9},{11,1... | collective-permute-start | bytes 221192 | tf_op jit(solution)/shard_map/ppermute | solution.py:26
where the time goes:
time: 170 us
  other arithmetic  52.7 us (31%)
  local copies, waits for them, and re-layouts  49.2 us (29%)
  waiting for transfers between devices  43.7 us (26%)
  starting transfers between devices  22.3 us (13%)
    all_to_all x1, waiting for transfers between devices, on_device(): lax.all_to_all(returning[:, source_slot], 'cols', split_axis=1, concat_ax...  25.5 us
    add x2, other arithmetic, crm_steps(): fields + STEP * (forcing[:, :, None, :] + MIXING * (sideways + vertical))  23.2 us
    all_to_all x1, waiting for transfers between devices, on_device(): lax.all_to_all(send_rows, 'cols', split_axis=1, concat_axis=1, tiled=True)  18.2 us
    slice x2, local copies, waits for them, and re-layouts, crm_steps(): jnp.roll(fields, -1, axis=2)  11.6 us
    another operation x4, other arithmetic, crm_steps(): fields = jnp.stack([fields[0] + LATENT * condensed, fields[1] - condensed])  10.6 us
    slice x2, local copies, waits for them, and re-layouts, crm_steps(): lower_cells = jnp.concatenate([fields[:, :1], fields[:, :-1]], axis=1)  7.31 us
    all_to_all x1, starting transfers between devices, on_device(): lax.all_to_all(send_labels, 'cols', split_axis=1, concat_axis=1, tiled=True)  7.3 us
    all_to_all x1, starting transfers between devices, on_device(): lax.all_to_all(send_rows, 'cols', split_axis=1, concat_axis=1, tiled=True)  5.83 us
  transfers between devices with their start and end apart: 5, of which 2 were waited for; matrix products, arithmetic and copies ran while one was open for 22% of the time, Pallas kernels for 0%

commit v1 on v0

--- a/solution.py
+++ b/solution.py
@@ -115,8 +115,14 @@
         "kj,fjc->fkc", interp_up, change, precision=lax.Precision.HIGHEST
     ).reshape(2 * LEV, columns)
     source_slot = jnp.minimum(arrived_slot, columns - 1)
-    returned = lax.all_to_all(
-        returning[:, source_slot], "cols", split_axis=1, concat_axis=1, tiled=True
+    returned = jnp.concatenate(
+        lax.all_to_all(
+            jnp.stack(jnp.split(returning[:, source_slot], lax.axis_size("cols"), axis=1)),
+            "cols",
+            0,
+            0,
+        ),
+        axis=1,
     )
     own_rows = returned[:, position]
     tendency = own_rows.reshape(2, LEV, columns)

time: 170 us -> 189 us (1.11)
  local copies, waits for them, and re-layouts: 49.2 us -> 67.7 us
    unnamed x11 -> x42, local copies, waits for them, and re-layouts: 2.02 us -> 21.1 us
  transfers between devices with their start and end apart: 5 -> 5, of which waited for: 2 -> 2; matrix products, arithmetic and copies ran while one was open for 22% -> 19% of each run, Pallas kernels for 0% -> 0%
where the time goes in v1:
time: 189 us; the launch traced here: 188 us
  local copies, waits for them, and re-layouts  67.7 us (36%)
  other arithmetic  52.7 us (28%)
  waiting for transfers between devices  43.9 us (23%)
  starting transfers between devices  22.1 us (12%)
    all_to_all x1, waiting for transfers between devices, on_device(): lax.all_to_all(jnp.stack(jnp.split(returning[:, source_slot], lax.axis_si...  25.7 us
    add x2, other arithmetic, crm_steps(): fields + STEP * (forcing[:, :, None, :] + MIXING * (sideways + vertical))  23.2 us
    unnamed x42, local copies, waits for them, and re-layouts  21.1 us
    all_to_all x1, waiting for transfers between devices, on_device(): lax.all_to_all(send_rows, 'cols', split_axis=1, concat_axis=1, tiled=True)  18.2 us
    slice x2, local copies, waits for them, and re-layouts, crm_steps(): jnp.roll(fields, -1, axis=2)  11.6 us
    another operation x4, other arithmetic, crm_steps(): fields = jnp.stack([fields[0] + LATENT * condensed, fields[1] - condensed])  10.6 us
    slice x2, local copies, waits for them, and re-layouts, crm_steps(): lower_cells = jnp.concatenate([fields[:, :1], fields[:, :-1]], axis=1)  7.31 us
    all_to_all x1, starting transfers between devices, on_device(): lax.all_to_all(send_labels, 'cols', split_axis=1, concat_axis=1, tiled=True)  7.3 us
  transfers between devices with their start and end apart: 5, of which 2 were waited for; matrix products, arithmetic and copies ran while one was open for 19% of the time, Pallas kernels for 0%

profile of v1, /device:TPU:0, one launch (start us, length us, event | category | flops | bytes accessed | tf_op | source)
XLA Modules:
  0.0 188.5 jit_solution(8146383987474895465)
XLA Ops:
  0.6 0.7 add_select_fusion.1
  1.3 1.2 reduce-window.6
  2.9 0.7 fusion.67
  3.7 1.0 copy.73
  4.8 1.9 %scatter_fusion = f32[2,1024]{0,1:T(8,128)S(1)} fusion(f32[2,1024]{0,1:T(8,128)S(1)} %copy.73, s32[512]{0:T(512)S(1)} %compare_select_fusion.4, f32[512,2]{1,0:T(8,128)S(1)} %copy.27), kind=kCustom, calls=%fused_computation.3 | custom fusion | bytes 14336 | tf_op jit(solution)/shard_map/scatter | solution.py:94
  6.7 0.9 copy.28
  7.6 7.3 %all-to-all-start = ((f32[2,32,32]{2,0,1:T(2,128)}), f32[2,32,32]{2,0,1:T(2,128)S(1)}, u32[]{:S(2)}, u32[]{:S(2)}) async-start(f32[2,32,32]{2,0,1:T(2,128)} %copy.28), calls=%async_computation | async-start | bytes 65536 | tf_op jit(solution)/shard_map/all_to_all | solution.py:97
  14.9 11.3 %fusion.79 = (f32[2,58,31,512]{3,2,1,0:T(8,128)}, f32[2,58,31,512]{3,2,1,0:T(8,128)}) fusion(bf16[2,58,32,512]{3,2,1,0:T(8,128)(2,1)} %param.6), kind=kLoop, calls=%fused_computation.225 | loop fusion | bytes 29458432 | tf_op jit(solution)/shard_map/jit(_roll_static)/slice | solution.py:46
  26.2 7.3 %fusion.78 = (f32[2,57,32,512]{3,2,1,0:T(8,128)}, f32[2,57,32,512]{3,2,1,0:T(8,128)}) fusion(bf16[2,58,32,512]{3,2,1,0:T(8,128)(2,1)S(1)} %copy-done), kind=kLoop, calls=%fused_computation.224 | loop fusion | bytes 29884416 | tf_op jit(solution)/shard_map/slice | solution.py:48
  34.1 3.3 %scatter_custom_fusion.1 = f32[144,1024]{0,1:T(8,128)} fusion(s32[512]{0:T(512)S(1)} %compare_select_fusion.4, f32[144,512]{0,1:T(8,128)S(1)} %copy.29, f32[]{:T(128)} %constant.56.clone.1), kind=kCustom, calls=%fused_computation.62 | custom fusion | bytes 1114116 | tf_op jit(solution)/shard_map/scatter | solution.py:89
  37.4 5.8 %all-to-all-start.1 = ((f32[144,32,32]{0,2,1:T(8,128)}), f32[144,32,32]{0,2,1:T(8,128)S(1)}, u32[]{:S(2)}, u32[]{:S(2)}) async-start(f32[144,32,32]{0,2,1:T(8,128)} %bitcast.9), calls=%async_computation.1 | async-start | bytes 2097152 | tf_op jit(solution)/shard_map/all_to_all | solution.py:96
  43.3 3.4 %convert_reduce_fusion = f32[2,58,512]{2,1,0:T(8,128)S(1)} fusion(bf16[2,58,32,512]{3,2,1,0:T(8,128)(2,1)} %param.6), kind=kLoop, calls=%fused_computation.55 | loop fusion | flops 3741696 | bytes 4038656 | tf_op jit(solution)/shard_map/reduce_sum | solution.py:58
  46.9 4.3 %scatter_custom_fusion.3 = s32[513]{0:T(1024)S(1)} fusion(s32[1024]{0:T(1024)S(1)} %bitcast.243, s32[1024]{0:T(1024)S(1)} %reshape.314, s32[]{:T(128)} %constant.62.clone.1), kind=kCustom, calls=%fused_computation.203 | custom fusion | bytes 2056 | tf_op jit(solution)/shard_map/scatter | solution.py:108
  51.3 18.2 %all-to-all-done.1 = f32[144,32,32]{0,2,1:T(8,128)S(1)} async-done(((f32[144,32,32]{0,2,1:T(8,128)}), f32[144,32,32]{0,2,1:T(8,128)S(1)}, u32[]{:S(2)}, u32[]{:S(2)}) %all-to-all-start.1) | async-done | bytes 589856 | tf_op jit(solution)/shard_map/all_to_all | solution.py:96
  69.5 5.1 %scatter_custom_fusion.2 = f32[144,513]{0,1:T(8,128)S(1)} fusion(s32[1024]{0:T(1024)S(1)} %bitcast.244, f32[1024,144]{1,0:T(8,128)S(1)} %bitcast.238, f32[]{:T(128)} %constant.56.clone.1), kind=kCustom, calls=%fused_computation.66 | custom fusion | bytes 295492 | tf_op jit(solution)/shard_map/scatter | solution.py:103
  75.2 13.5 %fusion.7 = f32[2,58,32,512]{3,2,1,0:T(8,128)S(1)} fusion(f32[2,58,31,512]{3,2,1,0:T(8,128)} %get-tuple-element.23, f32[2,58,1,512]{3,2,1,0:T(1,128)S(1)} %get-tuple-element.25, f32[2,58,1,512]{3,2,1,0:T(1,128)S(1)} %get-tuple-element.24, f32[2,58,31,512]{3,2,1,0:T(8,128)} %get-tuple-element.22, f32[2,1,32,512]{3,2,1,0:T(8,128)S(1)} %get-tuple-element.19, ...), kind=kLoop, calls=%fused_computation.32 | loop fusion | flops 28508160 | bytes 42049536 | tf_op jit(solution)/shard_map/add | solution.py:50
  88.8 1.5 fusion.21
  90.3 6.1 %fusion.17 = (f32[2,57,32,512]{3,2,1,0:T(8,128)}, f32[2,57,32,512]{3,2,1,0:T(8,128)}) fusion(f32[1,58,32,512]{3,2,1,0:T(8,128)S(1)} %get-tuple-element.9, f32[1,58,32,512]{3,2,1,0:T(8,128)S(1)} %get-tuple-element.8), kind=kLoop, calls=%fused_computation.46 | loop fusion | flops 3735552 | bytes 22544384 | tf_op jit(solution)/shard_map/stack | solution.py:52
  96.8 4.0 %fusion.1 = (f32[2,58,31,512]{3,2,1,0:T(8,128)S(1)}, f32[2,58,31,512]{3,2,1,0:T(8,128)}) fusion(f32[1,58,32,512]{3,2,1,0:T(8,128)S(1)} %get-tuple-element.9, f32[1,58,32,512]{3,2,1,0:T(8,128)S(1)} %get-tuple-element.8), kind=kLoop, calls=%fused_computation.25 | loop fusion | flops 3682304 | bytes 22331392 | tf_op jit(solution)/shard_map/stack | solution.py:52
  100.9 9.7 %fusion.14 = f32[2,58,32,512]{3,2,1,0:T(8,128)S(1)} fusion(f32[2,58,31,512]{3,2,1,0:T(8,128)} %get-tuple-element.15, f32[2,58,1,512]{3,2,1,0:T(1,128)S(1)} %get-tuple-element.17, f32[2,58,1,512]{3,2,1,0:T(1,128)S(1)} %get-tuple-element.16, f32[2,58,31,512]{3,2,1,0:T(8,128)S(1)} %get-tuple-element.14, f32[1,58,32,512]{3,2,1,0:T(8,128)S(1)} %get-tuple-element.8, ...), kind=kLoop, calls=%fused_computation.41 | loop fusion | flops 28508160 | bytes 45850624 | tf_op jit(solution)/shard_map/add | solution.py:50
  110.5 1.9 %slice_add_fusion = (f32[1,58,32,512]{3,2,1,0:T(8,128)S(1)}, f32[1,58,32,512]{3,2,1,0:T(8,128)S(1)}) fusion(f32[2,58,32,512]{3,2,1,0:T(8,128)S(1)} %fusion.14, f32[58,512]{1,0:T(8,128)S(1)} %fusion.40, f32[58]{0:T(128)S(1)} %multiply_subtract_fusion), kind=kLoop, calls=%fused_computation.49 | loop fusion | flops 5701632 | bytes 15323368 | tf_op jit(solution)/shard_map/add | solution.py:52
  112.5 1.5 fusion.18
  114.5 0.9 copy-done.2
  115.6 3.5 %gather_fusion = f32[1024,144]{1,0:T(8,128)S(1)} fusion(f32[144,512]{0,1:T(8,128)S(1)} %copy.31, s32[1024]{0:T(1024)S(1)} %broadcast_clamp_fusion.1), kind=kCustom, calls=%fused_computation | custom fusion | bytes 1183744 | tf_op jit(solution)/shard_map/gather | solution.py:120
  119.1 0.6 constant_dynamic-update-slice_fusion.31
  119.7 0.6 constant_dynamic-update-slice_fusion.30
  120.3 0.6 constant_dynamic-update-slice_fusion.29
  120.9 0.6 constant_dynamic-update-slice_fusion.28
  121.5 0.6 constant_dynamic-update-slice_fusion.27
  122.2 0.6 constant_dynamic-update-slice_fusion.26
  122.8 0.6 constant_dynamic-update-slice_fusion.25
  123.4 0.6 constant_dynamic-update-slice_fusion.24
  124.0 0.6 constant_dynamic-update-slice_fusion.23
  124.6 0.6 constant_dynamic-update-slice_fusion.22
  125.3 0.6 constant_dynamic-update-slice_fusion.21
  125.9 0.6 constant_dynamic-update-slice_fusion.20
  126.5 0.6 constant_dynamic-update-slice_fusion.19
  127.1 0.6 constant_dynamic-update-slice_fusion.18
  127.7 0.6 constant_dynamic-update-slice_fusion.17
  128.3 0.6 constant_dynamic-update-slice_fusion.16
  129.0 0.6 constant_dynamic-update-slice_fusion.15
  129.6 0.6 constant_dynamic-update-slice_fusion.14
  130.2 0.6 constant_dynamic-update-slice_fusion.13
  130.8 0.6 constant_dynamic-update-slice_fusion.12
  131.4 0.6 constant_dynamic-update-slice_fusion.11
  132.0 0.6 constant_dynamic-update-slice_fusion.10
  132.7 0.6 constant_dynamic-update-slice_fusion.9
  133.3 0.6 constant_dynamic-update-slice_fusion.8
  133.9 0.6 constant_dynamic-update-slice_fusion.7
  134.5 0.6 constant_dynamic-update-slice_fusion.6
  135.1 0.6 constant_dynamic-update-slice_fusion.5
  135.7 0.6 constant_dynamic-update-slice_fusion.4
  136.4 0.6 constant_dynamic-update-slice_fusion.3
  137.0 0.6 constant_dynamic-update-slice_fusion.2
  137.6 0.6 constant_dynamic-update-slice_fusion.1
  138.2 0.6 constant_dynamic-update-slice_fusion
  138.8 3.6 %all-to-all-start.2 = ((f32[32,144,32]{1,2,0:T(8,128)}), f32[32,144,32]{1,2,0:T(8,128)S(1)}, u32[]{:S(2)}, u32[]{:S(2)}) async-start(f32[32,144,32]{1,2,0:T(8,128)} %constant_dynamic-update-slice_fusion), calls=%async_computation.2 | async-start | bytes 2097152 | tf_op jit(solution)/shard_map/all_to_all | solution.py:119
  143.0 25.7 %all-to-all-done.2 = f32[32,144,32]{1,2,0:T(8,128)S(1)} async-done(((f32[32,144,32]{1,2,0:T(8,128)}), f32[32,144,32]{1,2,0:T(8,128)S(1)}, u32[]{:S(2)}, u32[]{:S(2)}) %all-to-all-start.2) | async-done | bytes 589856 | tf_op jit(solution)/shard_map/all_to_all | solution.py:119
  168.7 1.6 gather_fusion.1
  171.6 5.3 %collective-permute-start.1 = (f32[144,128]{0,1:T(8,128)S(1)}, f32[144,128]{0,1:T(8,128)S(1)}, u32[]{:S(2)}, u32[]{:S(2)}) collective-permute-start(f32[144,128]{0,1:T(8,128)S(1)} %broadcast_multiply_fusion), channel_id=1, source_target_pairs={{1,0},{2,1},{3,2},{4,3},{5,4},{6,5},{7,6},{8,7},{9,8},{10,9},{11,1... | collective-permute-start | bytes 221192 | tf_op jit(solution)/shard_map/ppermute | solution.py:26
  176.9 5.8 %fusion.19 = bf16[2,58,32,512]{3,2,1,0:T(8,128)(2,1)} fusion(f32[1,58,32,512]{3,2,1,0:T(8,128)} %copy-done.2, f32[1,58,32,512]{3,2,1,0:T(8,128)} %copy-done.1), kind=kLoop, calls=%fused_computation.48 | loop fusion | flops 1900544 | bytes 11403264 | tf_op jit(solution)/shard_map/convert_element_type | solution.py:64
  182.7 3.5 %gather_fusion.2 = f32[1024,144]{1,0:T(8,128)S(1)} fusion(f32[144,384]{0,1:T(8,128)S(1)} %pad_maximum_fusion.2, s32[1024]{0:T(1024)S(1)} %broadcast_clamp_fusion), kind=kCustom, calls=%fused_computation.2 | custom fusion | bytes 1183744 | tf_op jit(solution)/shard_map/jit(_take)/gather | solution.py:135
  186.2 0.7 fusion.25
  187.7 0.8 add.213
  (62 shorter events, 5.9 us)
Async XLA Ops:
  7.6 29.8 %all-to-all-start = ((f32[2,32,32]{2,0,1:T(2,128)}), f32[2,32,32]{2,0,1:T(2,128)S(1)}, u32[]{:S(2)}, u32[]{:S(2)}) async-start(f32[2,32,32]{2,0,1:T(2,128)} %copy.28), calls=%async_computation | async-start | bytes 65536 | tf_op jit(solution)/shard_map/all_to_all | solution.py:97
  14.9 11.3 %copy-start = (bf16[2,58,32,512]{3,2,1,0:T(8,128)(2,1)S(1)}, bf16[2,58,32,512]{3,2,1,0:T(8,128)(2,1)}, u32[]{:S(2)}) copy-start(bf16[2,58,32,512]{3,2,1,0:T(8,128)(2,1)} %param.6) | copy-start | bytes 11403268
  26.2 7.7 %copy-start.3 = (f32[2,72,512]{2,1,0:T(8,128)S(1)}, f32[2,72,512]{2,1,0:T(8,128)}, u32[]{:S(2)}) copy-start(f32[2,72,512]{2,1,0:T(8,128)} %param.5) | copy-start | bytes 884740
  37.4 32.1 %all-to-all-start.1 = ((f32[144,32,32]{0,2,1:T(8,128)}), f32[144,32,32]{0,2,1:T(8,128)S(1)}, u32[]{:S(2)}, u32[]{:S(2)}) async-start(f32[144,32,32]{0,2,1:T(8,128)} %bitcast.9), calls=%async_computation.1 | async-start | bytes 2097152 | tf_op jit(solution)/shard_map/all_to_all | solution.py:96
  112.4 2.0 %copy-start.1 = (f32[1,58,32,512]{3,2,1,0:T(8,128)}, f32[1,58,32,512]{3,2,1,0:T(8,128)S(1)}, u32[]{:S(2)}) copy-start(f32[1,58,32,512]{3,2,1,0:T(8,128)S(1)} %get-tuple-element.6) | copy-start | bytes 11403268
  112.5 2.9 %copy-start.2 = (f32[1,58,32,512]{3,2,1,0:T(8,128)}, f32[1,58,32,512]{3,2,1,0:T(8,128)S(1)}, u32[]{:S(2)}) copy-start(f32[1,58,32,512]{3,2,1,0:T(8,128)S(1)} %get-tuple-element.7) | copy-start | bytes 11403268
  112.5 30.0 %copy-start.4 = (s32[128,8]{0,1:T(8,128)S(1)}, s32[128,8]{0,1:T(8,128)}, u32[]{:S(2)}) copy-start(s32[128,8]{0,1:T(8,128)} %param.9) | copy-start | bytes 12292
  138.8 29.9 %all-to-all-start.2 = ((f32[32,144,32]{1,2,0:T(8,128)}), f32[32,144,32]{1,2,0:T(8,128)S(1)}, u32[]{:S(2)}, u32[]{:S(2)}) async-start(f32[32,144,32]{1,2,0:T(8,128)} %constant_dynamic-update-slice_fusion), calls=%async_computation.2 | async-start | bytes 2097152 | tf_op jit(solution)/shard_map/all_to_all | solution.py:119
  171.5 11.2 %collective-permute-start = (f32[144,128]{0,1:T(8,128)S(1)}, f32[144,128]{0,1:T(8,128)S(1)}, u32[]{:S(2)}, u32[]{:S(2)}) collective-permute-start(f32[144,128]{0,1:T(8,128)S(1)} %broadcast_multiply_fusion), channel_id=1, source_target_pairs={{0,1},{1,2},{2,3},{3,4},{4,5},{5,6},{6,7},{7,8},{8,9},{9,10},{10,1... | collective-permute-start | bytes 221192 | tf_op jit(solution)/shard_map/ppermute | solution.py:25
  171.6 11.1 %collective-permute-start.1 = (f32[144,128]{0,1:T(8,128)S(1)}, f32[144,128]{0,1:T(8,128)S(1)}, u32[]{:S(2)}, u32[]{:S(2)}) collective-permute-start(f32[144,128]{0,1:T(8,128)S(1)} %broadcast_multiply_fusion), channel_id=1, source_target_pairs={{1,0},{2,1},{3,2},{4,3},{5,4},{6,5},{7,6},{8,7},{9,8},{10,9},{11,1... | collective-permute-start | bytes 221192 | tf_op jit(solution)/shard_map/ppermute | solution.py:26
